TPU v7x, 256 devices: a whole 4x4x8 slice. The times are simulated.
256 devices in a mesh: gx: 32 (over z, x), gy: 4 (over y_lo, core), gz: 2 (over y_hi).
Axes of the slice: x: 4, y: 4 (y_hi: 2, y_lo: 2; y = y_hi * 2 + y_lo), z: 8, core: 2. Of those that a mesh axis runs over, the one named last changes fastest.
Arguments:
- coarse_fields: float32 [4, 512, 64, 256], P(None, 'gx', 'gy', 'gz'), may hold values from -6 to 6
- coarse_wind: float32 [3, 512, 64, 256], P(None, 'gx', 'gy', 'gz'), may hold values from -0.4 to 0.4
- fine_fields: float32 [4, 1024, 64, 256], P(None, 'gx', 'gy', 'gz'), may hold values from -6 to 6
- fine_wind: float32 [3, 1024, 64, 256], P(None, 'gx', 'gy', 'gz'), may hold values from -0.4 to 0.4
- fine_owner: int32 [32, 4, 2], P('gx', 'gy', 'gz'), may hold values from 0 to 31, as said below
Outputs:
- coarse_next: float32 [4, 512, 64, 256], P(None, 'gx', 'gy', 'gz')
- fine_next: float32 [4, 1024, 64, 256], P(None, 'gx', 'gy', 'gz')
Inputs may be any that keep to these rules, and one draw needn't show every extreme that they name: `fine_owner`: in each row of fine boxes along the first direction (fixed second and third index), fine box i refines coarse box (i + r) mod 32 for an offset r of that row, so every row names every coarse box once.
All inputs are finite; a program needn't handle non-finite values.
Results may differ from a plain program's by a relative error of at most 0.0003.
Values sent between devices are 32-bit elements; how exact they have to be, the bound alone decides.
A program may use at most 128 MiB of HBM per device.

v0:
```python
import math
import jax
import jax.numpy as jnp
from jax import lax
from jax.sharding import PartitionSpec as P

diffusion = 0.05
section_weights = (1.0 / 3.0, 0.5, 1.0)


def extended(array, sides, width, wrap):
    for axis, dim in sides:
        size, length = (lax.axis_size(axis), array.shape[dim])
        up = [(i, (i + 1) % size) for i in range(size if wrap else size - 1)]
        down = [(j, i) for i, j in up]
        last = lax.slice_in_dim(array, length - width, length, axis=dim)
        first = lax.slice_in_dim(array, 0, width, axis=dim)
        before = lax.ppermute(last, axis, up)
        after = lax.ppermute(first, axis, down)
        array = jnp.concatenate([before, array, after], axis=dim)
    return array


def tendency(padded, velocity):
    center = padded[:, 1:-1, 1:-1, 1:-1]
    along_first = padded[:, 2:, 1:-1, 1:-1] - padded[:, :-2, 1:-1, 1:-1]
    along_second = padded[:, 1:-1, 2:, 1:-1] - padded[:, 1:-1, :-2, 1:-1]
    along_third = padded[:, 1:-1, 1:-1, 2:] - padded[:, 1:-1, 1:-1, :-2]
    beside_all = (
        padded[:, 2:, 1:-1, 1:-1]
        + padded[:, :-2, 1:-1, 1:-1]
        + (padded[:, 1:-1, 2:, 1:-1] + padded[:, 1:-1, :-2, 1:-1])
        + (padded[:, 1:-1, 1:-1, 2:] + padded[:, 1:-1, 1:-1, :-2])
    )
    advect = velocity[0] * along_first + velocity[1] * along_second + velocity[2] * along_third
    return -0.5 * advect + diffusion * (beside_all - 6.0 * center)


def refine(coarse, direction):
    length = coarse.shape[direction]
    low_part = lax.slice_in_dim(coarse, 0, length - 1, axis=direction)
    high_part = lax.slice_in_dim(coarse, 1, length, axis=direction)
    odd_cells = 0.75 * low_part + 0.25 * high_part
    even_cells = 0.25 * low_part + 0.75 * high_part
    paired = jnp.stack((odd_cells, even_cells), axis=direction + 1)
    target = list(coarse.shape)
    target[direction] = 2 * (length - 1)
    return paired.reshape(target)


def coarse_slabs(padded, lead_y, span_y, lead_z, span_z):
    rows_y = jnp.concatenate(
        (padded[:, :, lead_y : lead_y + 2], padded[:, :, lead_y + span_y : lead_y + span_y + 2]),
        axis=2,
    )
    slab_y = rows_y[:, :, :, lead_z : lead_z + span_z + 2]
    rows_z = jnp.concatenate(
        (
            padded[:, :, :, lead_z : lead_z + 2],
            padded[:, :, :, lead_z + span_z : lead_z + span_z + 2],
        ),
        axis=3,
    )
    slab_z = rows_z[:, :, lead_y : lead_y + span_y + 2, :]
    return (slab_y, slab_z)


def slab_faces(slab_y, slab_z):
    wide_y = refine(slab_y, 1)[:, 1:-1]
    low_y = 0.75 * wide_y[:, :, 0] + 0.25 * wide_y[:, :, 1]
    high_y = 0.25 * wide_y[:, :, 2] + 0.75 * wide_y[:, :, 3]
    faces_y = refine(jnp.stack((low_y, high_y), axis=2), 3)[:, :, :, 1:-1]
    wide_z = refine(refine(slab_z, 1)[:, 1:-1], 2)[:, :, 1:-1]
    low_z = 0.75 * wide_z[:, :, :, 0] + 0.25 * wide_z[:, :, :, 1]
    high_z = 0.25 * wide_z[:, :, :, 2] + 0.75 * wide_z[:, :, :, 3]
    faces_z = jnp.stack((low_z, high_z), axis=3)
    return (faces_y, faces_z)


def fine_padded(widened, faces_y, faces_z):
    inner = widened[:, 1:-1]
    middle = jnp.concatenate((faces_z[:, :, :, 0:1], inner, faces_z[:, :, :, 1:2]), axis=3)
    side_low = jnp.pad(faces_y[:, :, 0:1], ((0, 0), (0, 0), (0, 0), (1, 1)))
    side_high = jnp.pad(faces_y[:, :, 1:2], ((0, 0), (0, 0), (0, 0), (1, 1)))
    middle = jnp.concatenate((side_low, middle, side_high), axis=2)
    end_low = jnp.pad(widened[:, 0:1], ((0, 0), (0, 0), (1, 1), (1, 1)))
    end_high = jnp.pad(widened[:, -1:], ((0, 0), (0, 0), (1, 1), (1, 1)))
    return jnp.concatenate((end_low, middle, end_high), axis=1)


def coarsen(fine):
    blocks = fine.reshape(
        fine.shape[0], fine.shape[1] // 2, 2, fine.shape[2] // 2, 2, fine.shape[3] // 2, 2
    )
    return 0.125 * jnp.sum(blocks, axis=(2, 4, 6))


def pack_parts(payload):
    return jnp.concatenate([member.reshape(member.shape[0], -1) for member in payload], axis=1)


def unpack_parts(packed, shapes):
    pieces = []
    cursor = 0
    for target in shapes:
        extent = math.prod(target[1:])
        pieces.append(packed[:, cursor : cursor + extent].reshape(target))
        cursor += extent
    return tuple(pieces)


def send_forward(payload, cycle_size, offset, position):
    shapes = [member.shape for member in payload]
    packed = pack_parts(payload)
    gathered = lax.all_gather(packed[None], "gx", axis=0, tiled=True)
    arrived = lax.dynamic_index_in_dim(
        gathered, (position + offset) % cycle_size, 0, keepdims=False
    )
    return unpack_parts(arrived, shapes)


def send_back(averaged, cycle_size, offset, position):
    packed = averaged.reshape(averaged.shape[0], -1)
    gathered = lax.all_gather(packed[None], "gx", axis=0, tiled=True)
    arrived = lax.dynamic_index_in_dim(
        gathered, (position - offset) % cycle_size, 0, keepdims=False
    )
    return arrived.reshape(averaged.shape)


def shards(coarse_fields, coarse_wind, fine_fields, fine_wind, fine_owner):
    cycle_size = lax.axis_size("gx")
    position = lax.axis_index("gx")
    offset = (fine_owner[0, 0, 0] - position) % cycle_size
    lead_y = coarse_fields.shape[2] // 4
    span_y = coarse_fields.shape[2] // 2
    lead_z = coarse_fields.shape[3] // 4
    span_z = coarse_fields.shape[3] // 2
    coarse_state = coarse_fields
    fine_state = fine_fields
    for fraction in section_weights:
        sides = extended(coarse_state, (("gx", 1), ("gy", 2)), 1, True)
        padded = extended(sides, (("gz", 3),), 1, False)
        coarse_rate = tendency(padded, coarse_wind)
        slab_y, slab_z = coarse_slabs(padded, lead_y, span_y, lead_z, span_z)
        faces_y, faces_z = slab_faces(slab_y, slab_z)
        faces_y, faces_z = send_forward((faces_y, faces_z), cycle_size, offset, position)
        widened = extended(fine_state, (("gx", 1),), 1, True)
        fine_rate = tendency(fine_padded(widened, faces_y, faces_z), fine_wind)
        coarse_state = coarse_fields + fraction * coarse_rate
        fine_state = fine_fields + fraction * fine_rate
    averaged = send_back(coarsen(fine_state), cycle_size, offset, position)
    column = jnp.concatenate(
        (
            coarse_state[:, :, lead_y : lead_y + span_y, :lead_z],
            averaged,
            coarse_state[:, :, lead_y : lead_y + span_y, lead_z + span_z :],
        ),
        axis=3,
    )
    coarse_next = jnp.concatenate(
        (coarse_state[:, :, :lead_y], column, coarse_state[:, :, lead_y + span_y :]), axis=2
    )
    return (coarse_next, fine_state)


def solution(mesh):
    return jax.shard_map(
        shards,
        mesh=mesh,
        in_specs=(
            P(None, "gx", "gy", "gz"),
            P(None, "gx", "gy", "gz"),
            P(None, "gx", "gy", "gz"),
            P(None, "gx", "gy", "gz"),
            P("gx", "gy", "gz"),
        ),
        out_specs=(P(None, "gx", "gy", "gz"), P(None, "gx", "gy", "gz")),
        check_vma=False,
    )
```

profile of v0, /device:TPU:8, one launch (start us, length us, event | category | flops | bytes accessed | tf_op | source)
XLA Modules:
  0.0 454.9 jit_solution(6036083444465853417)
XLA Ops:
  8.0 1.5 collective-permute-start.1
  9.5 6.6 %collective-permute-start = (f32[4,1,16,128]{3,2,1,0:T(8,128)S(1)}, f32[4,1,16,128]{3,2,1,0:T(8,128)S(1)}, u32[]{:S(2)}, u32[]{:S(2)}) collective-permute-start(f32[4,1,16,128]{3,2,1,0:T(8,128)S(1)} %get-tuple-element.55), channel_id=1, source_target_pairs={{8,0},{16,8},{24,16},{32,24},{40,32},{48,40},{56,48},{64,56},{72,6... | collective-permute-start | bytes 98312 | tf_op jit(solution)/shard_map/ppermute | solution.py:19
  16.1 1.8 collective-permute-done.1
  21.0 1.7 collective-permute-done.3
  22.9 1.5 fusion.29
  24.9 1.7 copy.594
  26.6 1.7 copy.592
  29.6 6.1 %collective-permute-start.5 = (f32[4,18,18,1]{2,0,3,1:T(4,128)S(1)}, f32[4,18,18,1]{2,0,3,1:T(4,128)S(1)}, u32[]{:S(2)}, u32[]{:S(2)}) collective-permute-start(f32[4,18,18,1]{2,0,3,1:T(4,128)S(1)} %copy.594), channel_id=1, source_target_pairs={{0,1},{2,3},{4,5},{6,7},{8,9},{10,11},{12,13},{14,15},{16,17},{18,... | collective-permute-start | bytes 15560 | tf_op jit(solution)/shard_map/ppermute | solution.py:18
  44.6 1.5 copy.595
  46.0 2.9 multiply_add_fusion.3
  49.0 5.3 %collective-permute-start.6 = (f32[4,1,16,128]{3,2,1,0:T(8,128)S(1)}, f32[4,1,16,128]{3,2,1,0:T(8,128)S(1)}, u32[]{:S(2)}, u32[]{:S(2)}) collective-permute-start(f32[4,1,16,128]{3,2,1,0:T(8,128)S(1)} %get-tuple-element.54), channel_id=1, source_target_pairs={{8,0},{16,8},{24,16},{32,24},{40,32},{48,40},{56,48},{64,56},{72,6... | collective-permute-start | bytes 98312 | tf_op jit(solution)/shard_map/ppermute | solution.py:19
  54.3 1.9 collective-permute-done.7
  58.1 1.8 collective-permute-done.9
  60.1 1.5 fusion.28
  61.5 2.3 copy.604
  63.8 2.3 copy.602
  67.4 7.3 %collective-permute-start.11 = (f32[4,18,18,1]{2,0,3,1:T(4,128)}, f32[4,18,18,1]{2,0,3,1:T(4,128)}, u32[]{:S(2)}, u32[]{:S(2)}) collective-permute-start(f32[4,18,18,1]{2,0,3,1:T(4,128)} %copy.604), channel_id=1, source_target_pairs={{0,1},{2,3},{4,5},{6,7},{8,9},{10,11},{12,13},{14,15},{16,17},{18,... | collective-permute-start | bytes 15560 | tf_op jit(solution)/shard_map/ppermute | solution.py:18
  77.0 2.2 copy.642
  90.5 2.2 copy.605
  92.7 2.0 multiply_add_fusion.2
  94.8 5.5 %collective-permute-start.12 = (f32[4,1,16,128]{3,2,1,0:T(8,128)S(1)}, f32[4,1,16,128]{3,2,1,0:T(8,128)S(1)}, u32[]{:S(2)}, u32[]{:S(2)}) collective-permute-start(f32[4,1,16,128]{3,2,1,0:T(8,128)S(1)} %get-tuple-element.52), channel_id=1, source_target_pairs={{8,0},{16,8},{24,16},{32,24},{40,32},{48,40},{56,48},{64,56},{72,6... | collective-permute-start | bytes 98312 | tf_op jit(solution)/shard_map/ppermute | solution.py:19
  100.3 1.9 collective-permute-done.13
  104.0 2.0 collective-permute-done.15
  107.4 2.3 copy.614
  112.1 6.7 %collective-permute-start.17 = (f32[4,18,18,1]{2,0,3,1:T(4,128)}, f32[4,18,18,1]{2,0,3,1:T(4,128)}, u32[]{:S(2)}, u32[]{:S(2)}) collective-permute-start(f32[4,18,18,1]{2,0,3,1:T(4,128)} %copy.614), channel_id=1, source_target_pairs={{0,1},{2,3},{4,5},{6,7},{8,9},{10,11},{12,13},{14,15},{16,17},{18,... | collective-permute-start | bytes 15560 | tf_op jit(solution)/shard_map/ppermute | solution.py:18
  124.4 1.4 copy.618
  131.1 5.4 %collective-permute-start.18 = (f32[4,1,16,128]{3,2,1,0:T(8,128)}, f32[4,1,16,128]{3,2,1,0:T(8,128)}, u32[]{:S(2)}, u32[]{:S(2)}) collective-permute-start(f32[4,1,16,128]{3,2,1,0:T(8,128)} %get-tuple-element.19), channel_id=1, source_target_pairs={{8,0},{16,8},{24,16},{32,24},{40,32},{48,40},{56,48},{64,56},{72,6... | collective-permute-start | bytes 98312 | tf_op jit(solution)/shard_map/ppermute | solution.py:19
  137.2 2.0 slice_bitcast_fusion.2
  139.3 69.0 %all-gather.15.cloned.1.call-done = f32[32,4,9216]{2,1,0:T(4,128)} async-done(((f32[1,4,9216]{2,1,0:T(4,128)}), f32[32,4,9216]{2,1,0:T(4,128)}) %all-gather.15.cloned.1.call-update) | async-done | bytes 4718608 | tf_op jit(solution)/shard_map/all_gather | solution.py:115
  214.2 4.7 %copy.664 = f32[4,32,16,1]{3,2,1,0:T(8,128)S(1)} copy(f32[4,32,16,1]{0,3,2,1:T(1,128)} %get-tuple-element.49) | data formatting | bytes 16384 | tf_op jit(solution)/shard_map/slice | solution.py:82
  218.9 5.6 %copy.665 = f32[4,32,16,1]{3,2,1,0:T(8,128)} copy(f32[4,32,16,1]{0,3,2,1:T(1,128)} %get-tuple-element.50) | data formatting | bytes 16384 | tf_op jit(solution)/shard_map/slice | solution.py:82
  224.5 4.7 %multiply_add_fusion.1 = f32[4,32,16,128]{3,2,1,0:T(8,128)S(1)} fusion(f32[4,32,16,128]{3,2,1,0:T(8,128)S(1)} %copy-done, f32[4,32,16,1]{3,2,1,0:T(8,128)} %copy.665, f32[4,32,16,1]{3,2,1,0:T(8,128)S(1)} %copy.664, f32[4,32,1,130]{3,2,1,0:T(1,128)} %pad.41, f32[4,32,1,130]{3,2,1,0:T(1,128)} %pad.40, f32[4,1,16,128]{3,2,1,0:T(8,128)} %collective-permute-done.18, ...), kind=kLoop, calls=%fused_computation.68 | loop fusion | flops 11534336 | bytes 3098624 | tf_op jit(solution)/shard_map/add | solution.py:151
  230.4 5.3 %collective-permute-start.20 = (f32[4,1,16,128]{3,2,1,0:T(8,128)S(1)}, f32[4,1,16,128]{3,2,1,0:T(8,128)}, u32[]{:S(2)}, u32[]{:S(2)}) collective-permute-start(f32[4,1,16,128]{3,2,1,0:T(8,128)S(1)} %get-tuple-element.17), channel_id=1, source_target_pairs={{8,0},{16,8},{24,16},{32,24},{40,32},{48,40},{56,48},{64,56},{72,6... | collective-permute-start | bytes 98312 | tf_op jit(solution)/shard_map/ppermute | solution.py:19
  237.6 4.7 %copy.668 = f32[4,32,16,1]{3,2,1,0:T(8,128)} copy(f32[4,32,16,1]{0,3,2,1:T(1,128)S(1)} %get-tuple-element.47) | data formatting | bytes 16384 | tf_op jit(solution)/shard_map/slice | solution.py:82
  242.2 4.7 %copy.669 = f32[4,32,16,1]{3,2,1,0:T(8,128)} copy(f32[4,32,16,1]{0,3,2,1:T(1,128)S(1)} %get-tuple-element.48) | data formatting | bytes 16384 | tf_op jit(solution)/shard_map/slice | solution.py:82
  247.5 7.4 %multiply_add_fusion = f32[4,32,16,128]{3,2,1,0:T(8,128)S(1)} fusion(f32[4,32,16,128]{3,2,1,0:T(8,128)S(1)} %copy-done, f32[4,32,16,128]{3,2,1,0:T(8,128)} %copy-done.2, f32[4,32,16,1]{3,2,1,0:T(8,128)} %copy.669, f32[4,32,16,1]{3,2,1,0:T(8,128)} %copy.668, f32[4,32,1,130]{3,2,1,0:T(1,128)} %pad.44, f32[4,32,1,130]{3,2,1,0:T(1,128)S(1)} %pad.39, ...), kind=kLoop, calls=%fused_computation.67 | loop fusion | flops 11534336 | bytes 4147200 | tf_op jit(solution)/shard_map/add | solution.py:151
  255.5 5.5 %collective-permute-start.22 = (f32[4,1,16,128]{3,2,1,0:T(8,128)}, f32[4,1,16,128]{3,2,1,0:T(8,128)}, u32[]{:S(2)}, u32[]{:S(2)}) collective-permute-start(f32[4,1,16,128]{3,2,1,0:T(8,128)} %get-tuple-element.15), channel_id=1, source_target_pairs={{8,0},{16,8},{24,16},{32,24},{40,32},{48,40},{56,48},{64,56},{72,6... | collective-permute-start | bytes 98312 | tf_op jit(solution)/shard_map/ppermute | solution.py:19
  261.1 29.9 %all-gather.13.cloned.1.call-done = f32[32,4,9216]{2,1,0:T(4,128)} async-done(((f32[1,4,9216]{2,1,0:T(4,128)}), f32[32,4,9216]{2,1,0:T(4,128)}) %all-gather.13.cloned.1.call-update) | async-done | bytes 4718608 | tf_op jit(solution)/shard_map/all_gather | solution.py:115
  294.7 2.6 fusion.33
  298.7 5.6 %copy.672 = f32[4,32,16,1]{3,2,1,0:T(8,128)} copy(f32[4,32,16,1]{0,3,2,1:T(1,128)} %get-tuple-element.45) | data formatting | bytes 16384 | tf_op jit(solution)/shard_map/slice | solution.py:82
  304.3 5.6 %copy.673 = f32[4,32,16,1]{3,2,1,0:T(8,128)} copy(f32[4,32,16,1]{0,3,2,1:T(1,128)} %get-tuple-element.46) | data formatting | bytes 16384 | tf_op jit(solution)/shard_map/slice | solution.py:82
  310.0 6.6 %add_add_fusion = f32[4,32,16,128]{3,2,1,0:T(8,128)} fusion(f32[4,32,16,128]{3,2,1,0:T(8,128)S(1)} %copy-done, f32[4,32,16,128]{3,2,1,0:T(8,128)S(1)} %multiply_add_fusion, f32[4,32,16,1]{3,2,1,0:T(8,128)} %copy.673, f32[4,32,16,1]{3,2,1,0:T(8,128)} %copy.672, f32[4,32,1,130]{3,2,1,0:T(1,128)} %pad.47, f32[4,32,1,130]{3,2,1,0:T(1,128)S(1)} %pad.38, ...), kind=kLoop, calls=%fused_computation.66 | loop fusion | flops 11272192 | bytes 4147200 | tf_op jit(solution)/shard_map/add | solution.py:151
  316.6 17.4 %copy.676 = f32[4,32,16,128]{0,3,2,1:T(8,128)} copy(f32[4,32,16,128]{3,2,1,0:T(8,128)} %add_add_fusion) | data formatting | bytes 2097152 | tf_op jit(solution)/shard_map/add | solution.py:151
  334.0 24.2 %reduce_sum.9 = f32[4,16,8,64]{0,3,2,1:T(8,128)} reduce(f32[4,16,2,8,2,64,2]{0,6,5,4,3,2,1:T(2,128)} %bitcast.106, f32[]{:T(128)} %constant.76.clone.1), dimensions={2,4,6}, to_apply=%region_0.1 | reduce | flops 229376 | bytes 1179652 | tf_op jit(solution)/shard_map/reduce_sum | solution.py:95
  358.2 5.0 %broadcast_multiply_fusion = f32[4,16,8,64]{0,3,2,1:T(8,128)} fusion(f32[4,16,8,64]{0,3,2,1:T(8,128)} %reduce_sum.9), kind=kLoop, calls=%fused_computation | loop fusion | flops 32768 | bytes 262144 | tf_op jit(solution)/shard_map/mul | solution.py:95
  363.2 3.6 copy.677
  367.4 1.3 copy.615
  369.8 76.1 %all-gather.11.cloned.1.call-done = f32[32,4,8192]{2,1,0:T(4,128)} async-done(((f32[1,4,8192]{2,1,0:T(4,128)}), f32[32,4,8192]{2,1,0:T(4,128)}) %all-gather.11.cloned.1.call-update) | async-done | bytes 4194320 | tf_op jit(solution)/shard_map/all_gather | solution.py:124
  (248 shorter events, 66.9 us)
Async XLA Ops:
  7.2 132.1 %all-gather.17.cloned.1.call-start = ((), (), s32[]{:S(2)}) async-start(), calls=%async_computation.3 | async-start | bytes 4866048 | tf_op jit(solution)/shard_map/all_gather | solution.py:115
  8.0 9.9 %collective-permute-start.1 = (f32[4,1,16,128]{3,2,1,0:T(8,128)S(1)}, f32[4,1,16,128]{3,2,1,0:T(8,128)S(1)}, u32[]{:S(2)}, u32[]{:S(2)}) collective-permute-start(f32[4,1,16,128]{3,2,1,0:T(8,128)S(1)} %get-tuple-element.56), channel_id=1, source_target_pairs={{0,8},{8,16},{16,24},{24,32},{32,40},{40,48},{48,56},{56,64},{64,7... | collective-permute-start | bytes 98312 | tf_op jit(solution)/shard_map/ppermute | solution.py:18
  9.5 9.5 %collective-permute-start = (f32[4,1,16,128]{3,2,1,0:T(8,128)S(1)}, f32[4,1,16,128]{3,2,1,0:T(8,128)S(1)}, u32[]{:S(2)}, u32[]{:S(2)}) collective-permute-start(f32[4,1,16,128]{3,2,1,0:T(8,128)S(1)} %get-tuple-element.55), channel_id=1, source_target_pairs={{8,0},{16,8},{24,16},{32,24},{40,32},{48,40},{56,48},{64,56},{72,6... | collective-permute-start | bytes 98312 | tf_op jit(solution)/shard_map/ppermute | solution.py:19
  19.1 1.8 collective-permute-start.2
  19.3 3.5 collective-permute-start.3
  28.3 11.6 %collective-permute-start.4 = (f32[4,18,18,1]{2,0,3,1:T(4,128)S(1)}, f32[4,18,18,1]{2,0,3,1:T(4,128)S(1)}, u32[]{:S(2)}, u32[]{:S(2)}) collective-permute-start(f32[4,18,18,1]{2,0,3,1:T(4,128)S(1)} %copy.592), channel_id=1, source_target_pairs={{1,0},{3,2},{5,4},{7,6},{9,8},{11,10},{13,12},{15,14},{17,16},{19,... | collective-permute-start | bytes 15560 | tf_op jit(solution)/shard_map/ppermute | solution.py:19
  29.6 9.7 %collective-permute-start.5 = (f32[4,18,18,1]{2,0,3,1:T(4,128)S(1)}, f32[4,18,18,1]{2,0,3,1:T(4,128)S(1)}, u32[]{:S(2)}, u32[]{:S(2)}) collective-permute-start(f32[4,18,18,1]{2,0,3,1:T(4,128)S(1)} %copy.594), channel_id=1, source_target_pairs={{0,1},{2,3},{4,5},{6,7},{8,9},{10,11},{12,13},{14,15},{16,17},{18,... | collective-permute-start | bytes 15560 | tf_op jit(solution)/shard_map/ppermute | solution.py:18
  43.7 164.6 %all-gather.15.cloned.1.call-start = ((), (), s32[]{:S(2)}) async-start(), calls=%async_computation.2 | async-start | bytes 4866048 | tf_op jit(solution)/shard_map/all_gather | solution.py:115
  44.0 48.7 %copy-start.5 = (f32[16,16,128]{2,1,0:T(8,128)}, f32[16,16,128]{2,1,0:T(8,128)S(1)}, u32[]{:S(2)}) copy-start(f32[16,16,128]{2,1,0:T(8,128)S(1)} %get-tuple-element.57) | copy-start | bytes 393220
  44.0 48.7 %copy-start.7 = (f32[16,16,128]{2,1,0:T(8,128)}, f32[16,16,128]{2,1,0:T(8,128)S(1)}, u32[]{:S(2)}) copy-start(f32[16,16,128]{2,1,0:T(8,128)S(1)} %get-tuple-element.58) | copy-start | bytes 393220
  44.0 48.7 %copy-start.9 = (f32[16,16,128]{2,1,0:T(8,128)}, f32[16,16,128]{2,1,0:T(8,128)S(1)}, u32[]{:S(2)}) copy-start(f32[16,16,128]{2,1,0:T(8,128)S(1)} %get-tuple-element.59) | copy-start | bytes 393220
  48.9 7.3 %collective-permute-start.7 = (f32[4,1,16,128]{3,2,1,0:T(8,128)S(1)}, f32[4,1,16,128]{3,2,1,0:T(8,128)S(1)}, u32[]{:S(2)}, u32[]{:S(2)}) collective-permute-start(f32[4,1,16,128]{3,2,1,0:T(8,128)S(1)} %get-tuple-element.53), channel_id=1, source_target_pairs={{0,8},{8,16},{16,24},{24,32},{32,40},{40,48},{48,56},{56,64},{64,7... | collective-permute-start | bytes 98312 | tf_op jit(solution)/shard_map/ppermute | solution.py:18
  49.0 7.2 %collective-permute-start.6 = (f32[4,1,16,128]{3,2,1,0:T(8,128)S(1)}, f32[4,1,16,128]{3,2,1,0:T(8,128)S(1)}, u32[]{:S(2)}, u32[]{:S(2)}) collective-permute-start(f32[4,1,16,128]{3,2,1,0:T(8,128)S(1)} %get-tuple-element.54), channel_id=1, source_target_pairs={{8,0},{16,8},{24,16},{32,24},{40,32},{48,40},{56,48},{64,56},{72,6... | collective-permute-start | bytes 98312 | tf_op jit(solution)/shard_map/ppermute | solution.py:19
  56.2 19.0 %copy-start.22 = (f32[4,1,16,128]{3,2,1,0:T(8,128)}, f32[4,1,16,128]{3,2,1,0:T(8,128)S(1)}, u32[]{:S(2)}) copy-start(f32[4,1,16,128]{3,2,1,0:T(8,128)S(1)} %collective-permute-done.7) | copy-start | bytes 98308
  56.2 19.0 %copy-start.24 = (f32[4,1,16,128]{3,2,1,0:T(8,128)}, f32[4,1,16,128]{3,2,1,0:T(8,128)S(1)}, u32[]{:S(2)}) copy-start(f32[4,1,16,128]{3,2,1,0:T(8,128)S(1)} %collective-permute-done.6) | copy-start | bytes 98308
  56.3 1.7 collective-permute-start.8
  56.4 3.5 collective-permute-start.9
  59.9 15.3 %copy-start.16 = (f32[4,18,1,128]{3,2,1,0:T(1,128)}, f32[4,18,1,128]{3,2,1,0:T(1,128)S(1)}, u32[]{:S(2)}) copy-start(f32[4,18,1,128]{3,2,1,0:T(1,128)S(1)} %copy.599) | copy-start | bytes 110596
  66.1 17.2 %collective-permute-start.10 = (f32[4,18,18,1]{2,0,3,1:T(4,128)}, f32[4,18,18,1]{2,0,3,1:T(4,128)}, u32[]{:S(2)}, u32[]{:S(2)}) collective-permute-start(f32[4,18,18,1]{2,0,3,1:T(4,128)} %copy.602), channel_id=1, source_target_pairs={{1,0},{3,2},{5,4},{7,6},{9,8},{11,10},{13,12},{15,14},{17,16},{19,... | collective-permute-start | bytes 15560 | tf_op jit(solution)/shard_map/ppermute | solution.py:19
  67.4 14.6 %collective-permute-start.11 = (f32[4,18,18,1]{2,0,3,1:T(4,128)}, f32[4,18,18,1]{2,0,3,1:T(4,128)}, u32[]{:S(2)}, u32[]{:S(2)}) collective-permute-start(f32[4,18,18,1]{2,0,3,1:T(4,128)} %copy.604), channel_id=1, source_target_pairs={{0,1},{2,3},{4,5},{6,7},{8,9},{10,11},{12,13},{14,15},{16,17},{18,... | collective-permute-start | bytes 15560 | tf_op jit(solution)/shard_map/ppermute | solution.py:18
  85.9 6.8 %copy-start.17 = (f32[4,18,1,128]{3,2,1,0:T(1,128)S(1)}, f32[4,18,1,128]{3,2,1,0:T(1,128)}, u32[]{:S(2)}) copy-start(f32[4,18,1,128]{3,2,1,0:T(1,128)} %copy-done.16) | copy-start | bytes 110596
  85.9 6.8 %copy-start.23 = (f32[4,1,16,128]{3,2,1,0:T(8,128)S(1)}, f32[4,1,16,128]{3,2,1,0:T(8,128)}, u32[]{:S(2)}) copy-start(f32[4,1,16,128]{3,2,1,0:T(8,128)} %copy-done.22) | copy-start | bytes 98308
  85.9 6.8 %copy-start.25 = (f32[4,1,16,128]{3,2,1,0:T(8,128)S(1)}, f32[4,1,16,128]{3,2,1,0:T(8,128)}, u32[]{:S(2)}) copy-start(f32[4,1,16,128]{3,2,1,0:T(8,128)} %copy-done.24) | copy-start | bytes 98308
  88.9 202.1 %all-gather.13.cloned.1.call-start = ((), (), s32[]{:S(2)}) async-start(), calls=%async_computation.1 | async-start | bytes 4866048 | tf_op jit(solution)/shard_map/all_gather | solution.py:115
  94.7 7.5 %collective-permute-start.13 = (f32[4,1,16,128]{3,2,1,0:T(8,128)S(1)}, f32[4,1,16,128]{3,2,1,0:T(8,128)S(1)}, u32[]{:S(2)}, u32[]{:S(2)}) collective-permute-start(f32[4,1,16,128]{3,2,1,0:T(8,128)S(1)} %get-tuple-element.51), channel_id=1, source_target_pairs={{0,8},{8,16},{16,24},{24,32},{32,40},{40,48},{48,56},{56,64},{64,7... | collective-permute-start | bytes 98312 | tf_op jit(solution)/shard_map/ppermute | solution.py:18
  94.8 7.4 %collective-permute-start.12 = (f32[4,1,16,128]{3,2,1,0:T(8,128)S(1)}, f32[4,1,16,128]{3,2,1,0:T(8,128)S(1)}, u32[]{:S(2)}, u32[]{:S(2)}) collective-permute-start(f32[4,1,16,128]{3,2,1,0:T(8,128)S(1)} %get-tuple-element.52), channel_id=1, source_target_pairs={{8,0},{16,8},{24,16},{32,24},{40,32},{48,40},{56,48},{64,56},{72,6... | collective-permute-start | bytes 98312 | tf_op jit(solution)/shard_map/ppermute | solution.py:19
  102.2 17.1 %copy-start.18 = (f32[4,1,16,128]{3,2,1,0:T(8,128)}, f32[4,1,16,128]{3,2,1,0:T(8,128)S(1)}, u32[]{:S(2)}) copy-start(f32[4,1,16,128]{3,2,1,0:T(8,128)S(1)} %collective-permute-done.13) | copy-start | bytes 98308
  102.2 17.1 %copy-start.20 = (f32[4,1,16,128]{3,2,1,0:T(8,128)}, f32[4,1,16,128]{3,2,1,0:T(8,128)S(1)}, u32[]{:S(2)}) copy-start(f32[4,1,16,128]{3,2,1,0:T(8,128)S(1)} %collective-permute-done.12) | copy-start | bytes 98308
  102.3 1.7 collective-permute-start.14
  102.4 3.6 collective-permute-start.15
  104.0 15.3 %copy-start.12 = (f32[4,18,1,128]{3,2,1,0:T(1,128)}, f32[4,18,1,128]{3,2,1,0:T(1,128)S(1)}, u32[]{:S(2)}) copy-start(f32[4,18,1,128]{3,2,1,0:T(1,128)S(1)} %copy.607) | copy-start | bytes 110596
  106.1 13.3 %copy-start.14 = (f32[4,18,1,128]{3,2,1,0:T(1,128)}, f32[4,18,1,128]{3,2,1,0:T(1,128)S(1)}, u32[]{:S(2)}) copy-start(f32[4,18,1,128]{3,2,1,0:T(1,128)S(1)} %copy.609) | copy-start | bytes 110596
  110.8 13.6 %collective-permute-start.16 = (f32[4,18,18,1]{2,0,3,1:T(4,128)}, f32[4,18,18,1]{2,0,3,1:T(4,128)S(1)}, u32[]{:S(2)}, u32[]{:S(2)}) collective-permute-start(f32[4,18,18,1]{2,0,3,1:T(4,128)} %copy.612), channel_id=1, source_target_pairs={{1,0},{3,2},{5,4},{7,6},{9,8},{11,10},{13,12},{15,14},{17,16},{19,... | collective-permute-start | bytes 15560 | tf_op jit(solution)/shard_map/ppermute | solution.py:19
  112.1 10.9 %collective-permute-start.17 = (f32[4,18,18,1]{2,0,3,1:T(4,128)}, f32[4,18,18,1]{2,0,3,1:T(4,128)}, u32[]{:S(2)}, u32[]{:S(2)}) collective-permute-start(f32[4,18,18,1]{2,0,3,1:T(4,128)} %copy.614), channel_id=1, source_target_pairs={{0,1},{2,3},{4,5},{6,7},{8,9},{10,11},{12,13},{14,15},{16,17},{18,... | collective-permute-start | bytes 15560 | tf_op jit(solution)/shard_map/ppermute | solution.py:18
  130.0 315.8 %all-gather.11.cloned.1.call-start = ((), (), s32[]{:S(2)}) async-start(), calls=%async_computation | async-start | bytes 4325376 | tf_op jit(solution)/shard_map/all_gather | solution.py:124
  130.7 93.8 %collective-permute-start.19 = (f32[4,1,16,128]{3,2,1,0:T(8,128)}, f32[4,1,16,128]{3,2,1,0:T(8,128)}, u32[]{:S(2)}, u32[]{:S(2)}) collective-permute-start(f32[4,1,16,128]{3,2,1,0:T(8,128)} %get-tuple-element.18), channel_id=1, source_target_pairs={{0,8},{8,16},{16,24},{24,32},{32,40},{40,48},{48,56},{56,64},{64,7... | collective-permute-start | bytes 98312 | tf_op jit(solution)/shard_map/ppermute | solution.py:18
  131.1 93.4 %collective-permute-start.18 = (f32[4,1,16,128]{3,2,1,0:T(8,128)}, f32[4,1,16,128]{3,2,1,0:T(8,128)}, u32[]{:S(2)}, u32[]{:S(2)}) collective-permute-start(f32[4,1,16,128]{3,2,1,0:T(8,128)} %get-tuple-element.19), channel_id=1, source_target_pairs={{8,0},{16,8},{24,16},{32,24},{40,32},{48,40},{56,48},{64,56},{72,6... | collective-permute-start | bytes 98312 | tf_op jit(solution)/shard_map/ppermute | solution.py:19
  224.5 11.2 %copy-start.4 = (f32[4,1024]{0,1:T(8,128)S(1)}, f32[4,1024]{0,1:T(8,128)}, u32[]{:S(2)}) copy-start(f32[4,1024]{0,1:T(8,128)} %copy.647) | copy-start | bytes 49156
  230.2 16.7 %collective-permute-start.21 = (f32[4,1,16,128]{3,2,1,0:T(8,128)S(1)}, f32[4,1,16,128]{3,2,1,0:T(8,128)S(1)}, u32[]{:S(2)}, u32[]{:S(2)}) collective-permute-start(f32[4,1,16,128]{3,2,1,0:T(8,128)S(1)} %get-tuple-element.16), channel_id=1, source_target_pairs={{0,8},{8,16},{16,24},{24,32},{32,40},{40,48},{48,56},{56,64},{64,7... | collective-permute-start | bytes 98312 | tf_op jit(solution)/shard_map/ppermute | solution.py:18
  230.4 17.1 %collective-permute-start.20 = (f32[4,1,16,128]{3,2,1,0:T(8,128)S(1)}, f32[4,1,16,128]{3,2,1,0:T(8,128)}, u32[]{:S(2)}, u32[]{:S(2)}) collective-permute-start(f32[4,1,16,128]{3,2,1,0:T(8,128)S(1)} %get-tuple-element.17), channel_id=1, source_target_pairs={{8,0},{16,8},{24,16},{32,24},{40,32},{48,40},{56,48},{64,56},{72,6... | collective-permute-start | bytes 98312 | tf_op jit(solution)/shard_map/ppermute | solution.py:19
  255.5 54.4 %collective-permute-start.23 = (f32[4,1,16,128]{3,2,1,0:T(8,128)}, f32[4,1,16,128]{3,2,1,0:T(8,128)}, u32[]{:S(2)}, u32[]{:S(2)}) collective-permute-start(f32[4,1,16,128]{3,2,1,0:T(8,128)} %get-tuple-element.14), channel_id=1, source_target_pairs={{0,8},{8,16},{16,24},{24,32},{32,40},{40,48},{48,56},{56,64},{64,7... | collective-permute-start | bytes 98312 | tf_op jit(solution)/shard_map/ppermute | solution.py:18
  255.5 54.4 %collective-permute-start.22 = (f32[4,1,16,128]{3,2,1,0:T(8,128)}, f32[4,1,16,128]{3,2,1,0:T(8,128)}, u32[]{:S(2)}, u32[]{:S(2)}) collective-permute-start(f32[4,1,16,128]{3,2,1,0:T(8,128)} %get-tuple-element.15), channel_id=1, source_target_pairs={{8,0},{16,8},{24,16},{32,24},{40,32},{48,40},{56,48},{64,56},{72,6... | collective-permute-start | bytes 98312 | tf_op jit(solution)/shard_map/ppermute | solution.py:19
  363.1 5.6 %copy-start.8 = (f32[16,16,128]{2,1,0:T(8,128)S(1)}, f32[16,16,128]{2,1,0:T(8,128)}, u32[]{:S(2)}) copy-start(f32[16,16,128]{2,1,0:T(8,128)} %copy-done.7) | copy-start | bytes 393220
  363.1 5.6 %copy-start.10 = (f32[16,16,128]{2,1,0:T(8,128)S(1)}, f32[16,16,128]{2,1,0:T(8,128)}, u32[]{:S(2)}) copy-start(f32[16,16,128]{2,1,0:T(8,128)} %copy-done.9) | copy-start | bytes 393220
  363.1 5.6 %copy-start.13 = (f32[4,18,1,128]{3,2,1,0:T(1,128)S(1)}, f32[4,18,1,128]{3,2,1,0:T(1,128)}, u32[]{:S(2)}) copy-start(f32[4,18,1,128]{3,2,1,0:T(1,128)} %copy-done.12) | copy-start | bytes 110596
  363.2 5.6 %copy-start.15 = (f32[4,18,1,128]{3,2,1,0:T(1,128)S(1)}, f32[4,18,1,128]{3,2,1,0:T(1,128)}, u32[]{:S(2)}) copy-start(f32[4,18,1,128]{3,2,1,0:T(1,128)} %copy-done.14) | copy-start | bytes 110596
  363.2 5.6 %copy-start.19 = (f32[4,1,16,128]{3,2,1,0:T(8,128)S(1)}, f32[4,1,16,128]{3,2,1,0:T(8,128)}, u32[]{:S(2)}) copy-start(f32[4,1,16,128]{3,2,1,0:T(8,128)} %copy-done.18) | copy-start | bytes 98308
  363.2 5.6 %copy-start.21 = (f32[4,1,16,128]{3,2,1,0:T(8,128)S(1)}, f32[4,1,16,128]{3,2,1,0:T(8,128)}, u32[]{:S(2)}) copy-start(f32[4,1,16,128]{3,2,1,0:T(8,128)} %copy-done.20) | copy-start | bytes 98308
  (9 other events, 32.3 us)
Sparse Core Ops, SparseCore 0:
  43.8 82.2 all-gather.16
  128.7 79.5 all-gather.14
  210.9 80.0 all-gather.12
  366.9 78.9 all-gather.10
where the time goes:
time: 464 us; the launch traced here: 455 us
  waiting for transfers between devices  189 us (41%)
  local copies, waits for them, and re-layouts  119 us (26%)
  other arithmetic  68.2 us (15%)
  starting transfers between devices  62.3 us (13%)
  between operations  15.8 us (3%)
    all_gather x3, waiting for transfers between devices, send_forward(): gathered = lax.all_gather(packed[None], 'gx', axis=0, tiled=True)  98.9 us
    all_gather x1, waiting for transfers between devices, send_back(): gathered = lax.all_gather(packed[None], 'gx', axis=0, tiled=True)  76.1 us
    ppermute x12, starting transfers between devices, extended(): after = lax.ppermute(first, axis, down)  37.8 us
    reduce_sum x1, other arithmetic, coarsen(): return 0.125 * jnp.sum(blocks, axis=(2, 4, 6))  24.2 us
    ppermute x12, starting transfers between devices, extended(): before = lax.ppermute(last, axis, up)  23.9 us
    slice x6, local copies, waits for them, and re-layouts, fine_padded(): faces_z[:, :, :, 0:1]  19.2 us
    add x3, other arithmetic, shards(): fine_state = fine_fields + fraction * fine_rate  18.7 us
    add x1, local copies, waits for them, and re-layouts, shards(): fine_state = fine_fields + fraction * fine_rate  17.4 us
  transfers between devices with their start and end apart: 28, of which 12 were waited for; matrix products, arithmetic and copies ran while one was open for 26% of the time, Pallas kernels for 0%

commit v1 on v0

--- a/solution.py
+++ b/solution.py
@@ -121,7 +121,9 @@
 
 def send_back(averaged, cycle_size, offset, position):
     packed = averaged.reshape(averaged.shape[0], -1)
-    gathered = lax.all_gather(packed[None], "gx", axis=0, tiled=True)
+    gathered = jnp.concatenate(
+        lax.all_to_all(jnp.stack([packed[None]] * lax.axis_size("gx")), "gx", 0, 0), axis=0
+    )
     arrived = lax.dynamic_index_in_dim(
         gathered, (position - offset) % cycle_size, 0, keepdims=False
     )

time: 464 us -> 489 us (1.054)
  waiting for transfers between devices: 189 us -> 208 us
    all_to_all x0 -> x1, waiting for transfers between devices: none -> 89.4 us  [send_back(): lax.all_to_all(jnp.stack([packed[None]] * lax.axis_size('gx')), 'gx', 0, 0)]
    all_gather x1 -> x0, waiting for transfers between devices: 76.1 us -> none  [send_back(): gathered = lax.all_gather(packed[None], 'gx', axis=0, tiled=True)]
    all_to_all x0 -> x1, starting transfers between devices: none -> 5.7 us  [send_back(): lax.all_to_all(jnp.stack([packed[None]] * lax.axis_size('gx')), 'gx', 0, 0)]
    all_gather x3, waiting for transfers between devices: 98.9 us -> 104 us  [send_forward(): gathered = lax.all_gather(packed[None], 'gx', axis=0, tiled=True)]
  transfers between devices with their start and end apart: 28 -> 28, of which waited for: 12 -> 14; matrix products, arithmetic and copies ran while one was open for 26% -> 24% of each run, Pallas kernels for 0% -> 0%
where the time goes in v1:
time: 489 us; the launch traced here: 480 us
  waiting for transfers between devices  208 us (43%)
  local copies, waits for them, and re-layouts  122 us (25%)
  other arithmetic  67.6 us (14%)
  starting transfers between devices  67 us (14%)
  between operations  15.9 us (3%)
    all_gather x3, waiting for transfers between devices, send_forward(): gathered = lax.all_gather(packed[None], 'gx', axis=0, tiled=True)  104 us
    all_to_all x1, waiting for transfers between devices, send_back(): lax.all_to_all(jnp.stack([packed[None]] * lax.axis_size('gx')), 'gx', 0, 0)  89.4 us
    ppermute x12, starting transfers between devices, extended(): after = lax.ppermute(first, axis, down)  38.7 us
    reduce_sum x1, other arithmetic, coarsen(): return 0.125 * jnp.sum(blocks, axis=(2, 4, 6))  24.2 us
    ppermute x12, starting transfers between devices, extended(): before = lax.ppermute(last, axis, up)  21.9 us
    slice x6, local copies, waits for them, and re-layouts, fine_padded(): faces_z[:, :, :, 0:1]  19.2 us
    add x3, other arithmetic, shards(): fine_state = fine_fields + fraction * fine_rate  18.9 us
    add x1, local copies, waits for them, and re-layouts, shards(): fine_state = fine_fields + fraction * fine_rate  17.4 us
  transfers between devices with their start and end apart: 28, of which 14 were waited for; matrix products, arithmetic and copies ran while one was open for 24% of the time, Pallas kernels for 0%

profile of v1, /device:TPU:8, one launch (start us, length us, event | category | flops | bytes accessed | tf_op | source)
XLA Modules:
  0.0 480.2 jit_solution(2495319471081327119)
XLA Ops:
  8.0 1.5 collective-permute-start.1
  9.5 6.6 %collective-permute-start = (f32[4,1,16,128]{3,2,1,0:T(8,128)S(1)}, f32[4,1,16,128]{3,2,1,0:T(8,128)S(1)}, u32[]{:S(2)}, u32[]{:S(2)}) collective-permute-start(f32[4,1,16,128]{3,2,1,0:T(8,128)S(1)} %get-tuple-element.55), channel_id=1, source_target_pairs={{8,0},{16,8},{24,16},{32,24},{40,32},{48,40},{56,48},{64,56},{72,6... | collective-permute-start | bytes 98312 | tf_op jit(solution)/shard_map/ppermute | solution.py:19
  16.1 1.8 collective-permute-done.1
  22.2 1.7 collective-permute-done.3
  26.4 2.3 copy.594
  31.2 6.0 %collective-permute-start.5 = (f32[4,18,18,1]{2,0,3,1:T(4,128)}, f32[4,18,18,1]{2,0,3,1:T(4,128)S(1)}, u32[]{:S(2)}, u32[]{:S(2)}) collective-permute-start(f32[4,18,18,1]{2,0,3,1:T(4,128)} %copy.594), channel_id=1, source_target_pairs={{0,1},{2,3},{4,5},{6,7},{8,9},{10,11},{12,13},{14,15},{16,17},{18,... | collective-permute-start | bytes 15560 | tf_op jit(solution)/shard_map/ppermute | solution.py:18
  45.6 1.8 slice_bitcast_fusion.5
  48.5 1.9 multiply_add_fusion.3
  50.6 5.3 %collective-permute-start.6 = (f32[4,1,16,128]{3,2,1,0:T(8,128)S(1)}, f32[4,1,16,128]{3,2,1,0:T(8,128)S(1)}, u32[]{:S(2)}, u32[]{:S(2)}) collective-permute-start(f32[4,1,16,128]{3,2,1,0:T(8,128)S(1)} %get-tuple-element.54), channel_id=1, source_target_pairs={{8,0},{16,8},{24,16},{32,24},{40,32},{48,40},{56,48},{64,56},{72,6... | collective-permute-start | bytes 98312 | tf_op jit(solution)/shard_map/ppermute | solution.py:19
  55.9 1.9 collective-permute-done.7
  59.7 1.8 collective-permute-done.9
  63.5 2.3 copy.604
  68.2 6.0 %collective-permute-start.11 = (f32[4,18,18,1]{2,0,3,1:T(4,128)}, f32[4,18,18,1]{2,0,3,1:T(4,128)S(1)}, u32[]{:S(2)}, u32[]{:S(2)}) collective-permute-start(f32[4,18,18,1]{2,0,3,1:T(4,128)} %copy.604), channel_id=1, source_target_pairs={{0,1},{2,3},{4,5},{6,7},{8,9},{10,11},{12,13},{14,15},{16,17},{18,... | collective-permute-start | bytes 15560 | tf_op jit(solution)/shard_map/ppermute | solution.py:18
  85.2 1.9 multiply_add_fusion.2
  87.2 5.9 %collective-permute-start.12 = (f32[4,1,16,128]{3,2,1,0:T(8,128)S(1)}, f32[4,1,16,128]{3,2,1,0:T(8,128)S(1)}, u32[]{:S(2)}, u32[]{:S(2)}) collective-permute-start(f32[4,1,16,128]{3,2,1,0:T(8,128)S(1)} %get-tuple-element.52), channel_id=1, source_target_pairs={{8,0},{16,8},{24,16},{32,24},{40,32},{48,40},{56,48},{64,56},{72,6... | collective-permute-start | bytes 98312 | tf_op jit(solution)/shard_map/ppermute | solution.py:19
  93.1 1.8 collective-permute-done.13
  97.0 1.8 collective-permute-done.15
  100.2 1.7 copy.614
  103.8 6.1 %collective-permute-start.17 = (f32[4,18,18,1]{2,0,3,1:T(4,128)S(1)}, f32[4,18,18,1]{2,0,3,1:T(4,128)S(1)}, u32[]{:S(2)}, u32[]{:S(2)}) collective-permute-start(f32[4,18,18,1]{2,0,3,1:T(4,128)S(1)} %copy.614), channel_id=1, source_target_pairs={{0,1},{2,3},{4,5},{6,7},{8,9},{10,11},{12,13},{14,15},{16,17},{18,... | collective-permute-start | bytes 15560 | tf_op jit(solution)/shard_map/ppermute | solution.py:18
  112.2 2.2 copy.625
  116.4 1.4 copy.616
  118.4 1.4 copy.618
  119.7 1.4 pad_maximum_fusion.118
  124.9 5.9 %collective-permute-start.18 = (f32[4,1,16,128]{3,2,1,0:T(8,128)}, f32[4,1,16,128]{3,2,1,0:T(8,128)}, u32[]{:S(2)}, u32[]{:S(2)}) collective-permute-start(f32[4,1,16,128]{3,2,1,0:T(8,128)} %get-tuple-element.19), channel_id=1, source_target_pairs={{8,0},{16,8},{24,16},{32,24},{40,32},{48,40},{56,48},{64,56},{72,6... | collective-permute-start | bytes 98312 | tf_op jit(solution)/shard_map/ppermute | solution.py:19
  131.4 2.0 slice_bitcast_fusion.2
  133.4 75.9 %all-gather.12.cloned.1.call-done = f32[32,4,9216]{2,1,0:T(4,128)} async-done(((f32[1,4,9216]{2,1,0:T(4,128)}), f32[32,4,9216]{2,1,0:T(4,128)}) %all-gather.12.cloned.1.call-update) | async-done | bytes 4718608 | tf_op jit(solution)/shard_map/all_gather | solution.py:115
  215.9 4.7 copy.664
  220.6 5.6 %copy.665 = f32[4,32,16,1]{3,2,1,0:T(8,128)} copy(f32[4,32,16,1]{0,3,2,1:T(1,128)} %get-tuple-element.50) | data formatting | bytes 16384 | tf_op jit(solution)/shard_map/slice | solution.py:82
  226.2 4.7 multiply_add_fusion.1
  232.2 5.3 %collective-permute-start.20 = (f32[4,1,16,128]{3,2,1,0:T(8,128)S(1)}, f32[4,1,16,128]{3,2,1,0:T(8,128)}, u32[]{:S(2)}, u32[]{:S(2)}) collective-permute-start(f32[4,1,16,128]{3,2,1,0:T(8,128)S(1)} %get-tuple-element.17), channel_id=1, source_target_pairs={{8,0},{16,8},{24,16},{32,24},{40,32},{48,40},{56,48},{64,56},{72,6... | collective-permute-start | bytes 98312 | tf_op jit(solution)/shard_map/ppermute | solution.py:19
  241.0 4.7 copy.668
  245.6 4.7 copy.669
  250.3 7.5 %multiply_add_fusion = f32[4,32,16,128]{3,2,1,0:T(8,128)S(1)} fusion(f32[4,32,16,128]{3,2,1,0:T(8,128)S(1)} %copy-done, f32[4,32,16,128]{3,2,1,0:T(8,128)} %copy-done.2, f32[4,32,16,1]{3,2,1,0:T(8,128)} %copy.669, f32[4,32,16,1]{3,2,1,0:T(8,128)} %copy.668, f32[4,32,1,130]{3,2,1,0:T(1,128)} %pad.44, f32[4,32,1,130]{3,2,1,0:T(1,128)} %pad.39, ...), kind=kLoop, calls=%fused_computation.67 | loop fusion | flops 11534336 | bytes 4147200 | tf_op jit(solution)/shard_map/add | solution.py:153
  258.5 5.6 %collective-permute-start.22 = (f32[4,1,16,128]{3,2,1,0:T(8,128)}, f32[4,1,16,128]{3,2,1,0:T(8,128)}, u32[]{:S(2)}, u32[]{:S(2)}) collective-permute-start(f32[4,1,16,128]{3,2,1,0:T(8,128)} %get-tuple-element.15), channel_id=1, source_target_pairs={{8,0},{16,8},{24,16},{32,24},{40,32},{48,40},{56,48},{64,56},{72,6... | collective-permute-start | bytes 98312 | tf_op jit(solution)/shard_map/ppermute | solution.py:19
  264.0 28.3 %all-gather.10.cloned.1.call-done = f32[32,4,9216]{2,1,0:T(4,128)} async-done(((f32[1,4,9216]{2,1,0:T(4,128)}), f32[32,4,9216]{2,1,0:T(4,128)}) %all-gather.10.cloned.1.call-update) | async-done | bytes 4718608 | tf_op jit(solution)/shard_map/all_gather | solution.py:115
  293.9 1.7 reshape.102
  296.6 2.6 fusion.33
  302.4 5.6 %copy.672 = f32[4,32,16,1]{3,2,1,0:T(8,128)} copy(f32[4,32,16,1]{0,3,2,1:T(1,128)} %get-tuple-element.45) | data formatting | bytes 16384 | tf_op jit(solution)/shard_map/slice | solution.py:82
  308.0 5.6 %copy.673 = f32[4,32,16,1]{3,2,1,0:T(8,128)} copy(f32[4,32,16,1]{0,3,2,1:T(1,128)} %get-tuple-element.46) | data formatting | bytes 16384 | tf_op jit(solution)/shard_map/slice | solution.py:82
  313.6 6.7 %add_add_fusion = f32[4,32,16,128]{3,2,1,0:T(8,128)} fusion(f32[4,32,16,128]{3,2,1,0:T(8,128)S(1)} %copy-done, f32[4,32,16,128]{3,2,1,0:T(8,128)S(1)} %multiply_add_fusion, f32[4,32,16,1]{3,2,1,0:T(8,128)} %copy.673, f32[4,32,16,1]{3,2,1,0:T(8,128)} %copy.672, f32[4,32,1,130]{3,2,1,0:T(1,128)} %pad.47, f32[4,32,1,130]{3,2,1,0:T(1,128)} %pad.38, ...), kind=kLoop, calls=%fused_computation.66 | loop fusion | flops 11272192 | bytes 4147200 | tf_op jit(solution)/shard_map/add | solution.py:153
  320.3 17.4 %copy.676 = f32[4,32,16,128]{0,3,2,1:T(8,128)} copy(f32[4,32,16,128]{3,2,1,0:T(8,128)} %add_add_fusion) | data formatting | bytes 2097152 | tf_op jit(solution)/shard_map/add | solution.py:153
  337.7 24.2 %reduce_sum.9 = f32[4,16,8,64]{0,3,2,1:T(8,128)} reduce(f32[4,16,2,8,2,64,2]{0,6,5,4,3,2,1:T(2,128)} %bitcast.106, f32[]{:T(128)} %constant.77.clone.1), dimensions={2,4,6}, to_apply=%region_0.1 | reduce | flops 229376 | bytes 1179652 | tf_op jit(solution)/shard_map/reduce_sum | solution.py:95
  361.9 5.0 %broadcast_multiply_fusion = f32[4,16,8,64]{0,3,2,1:T(8,128)} fusion(f32[4,16,8,64]{0,3,2,1:T(8,128)} %reduce_sum.9), kind=kLoop, calls=%fused_computation | loop fusion | flops 32768 | bytes 262144 | tf_op jit(solution)/shard_map/mul | solution.py:95
  366.8 2.8 copy.677
  369.7 3.0 stack.183
  372.6 5.7 %all-to-all-start = ((f32[32,1,4,8192]{3,2,1,0:T(4,128)}), f32[32,1,4,8192]{3,2,1,0:T(4,128)}, u32[]{:S(2)}, u32[]{:S(2)}) async-start(f32[32,1,4,8192]{3,2,1,0:T(4,128)} %stack.183), calls=%async_computation | async-start | bytes 8388608 | tf_op jit(solution)/shard_map/all_to_all | solution.py:125
  379.5 1.8 add_add_fusion.1
  381.6 89.4 %all-to-all-done = f32[32,1,4,8192]{3,2,1,0:T(4,128)} async-done(((f32[32,1,4,8192]{3,2,1,0:T(4,128)}), f32[32,1,4,8192]{3,2,1,0:T(4,128)}, u32[]{:S(2)}, u32[]{:S(2)}) %all-to-all-start) | async-done | bytes 4194336 | tf_op jit(solution)/shard_map/all_to_all | solution.py:125
  (250 shorter events, 71.3 us)
Async XLA Ops:
  7.2 126.2 %all-gather.14.cloned.1.call-start = ((), (), s32[]{:S(2)}) async-start(), calls=%async_computation.3 | async-start | bytes 4866048 | tf_op jit(solution)/shard_map/all_gather | solution.py:115
  8.0 9.9 %collective-permute-start.1 = (f32[4,1,16,128]{3,2,1,0:T(8,128)S(1)}, f32[4,1,16,128]{3,2,1,0:T(8,128)S(1)}, u32[]{:S(2)}, u32[]{:S(2)}) collective-permute-start(f32[4,1,16,128]{3,2,1,0:T(8,128)S(1)} %get-tuple-element.56), channel_id=1, source_target_pairs={{0,8},{8,16},{16,24},{24,32},{32,40},{40,48},{48,56},{56,64},{64,7... | collective-permute-start | bytes 98312 | tf_op jit(solution)/shard_map/ppermute | solution.py:18
  9.5 10.1 %collective-permute-start = (f32[4,1,16,128]{3,2,1,0:T(8,128)S(1)}, f32[4,1,16,128]{3,2,1,0:T(8,128)S(1)}, u32[]{:S(2)}, u32[]{:S(2)}) collective-permute-start(f32[4,1,16,128]{3,2,1,0:T(8,128)S(1)} %get-tuple-element.55), channel_id=1, source_target_pairs={{8,0},{16,8},{24,16},{32,24},{40,32},{48,40},{56,48},{64,56},{72,6... | collective-permute-start | bytes 98312 | tf_op jit(solution)/shard_map/ppermute | solution.py:19
  20.2 3.7 copy-start.3
  20.3 1.8 collective-permute-start.2
  20.4 3.5 collective-permute-start.3
  29.9 11.6 %collective-permute-start.4 = (f32[4,18,18,1]{2,0,3,1:T(4,128)}, f32[4,18,18,1]{2,0,3,1:T(4,128)S(1)}, u32[]{:S(2)}, u32[]{:S(2)}) collective-permute-start(f32[4,18,18,1]{2,0,3,1:T(4,128)} %copy.592), channel_id=1, source_target_pairs={{1,0},{3,2},{5,4},{7,6},{9,8},{11,10},{13,12},{15,14},{17,16},{19,... | collective-permute-start | bytes 15560 | tf_op jit(solution)/shard_map/ppermute | solution.py:19
  31.2 9.8 %collective-permute-start.5 = (f32[4,18,18,1]{2,0,3,1:T(4,128)}, f32[4,18,18,1]{2,0,3,1:T(4,128)S(1)}, u32[]{:S(2)}, u32[]{:S(2)}) collective-permute-start(f32[4,18,18,1]{2,0,3,1:T(4,128)} %copy.594), channel_id=1, source_target_pairs={{0,1},{2,3},{4,5},{6,7},{8,9},{10,11},{12,13},{14,15},{16,17},{18,... | collective-permute-start | bytes 15560 | tf_op jit(solution)/shard_map/ppermute | solution.py:18
  41.0 2.7 copy-start.24
  42.5 6.0 %copy-start.1 = (f32[4,16,16,128]{3,2,1,0:T(8,128)S(1)}, f32[4,16,16,128]{3,2,1,0:T(8,128)}, u32[]{:S(2)}) copy-start(f32[4,16,16,128]{3,2,1,0:T(8,128)} %param.5) | copy-start | bytes 1572868
  42.6 6.0 %copy-start.4 = (f32[4,18,16,128]{3,2,1,0:T(8,128)S(1)}, f32[4,18,16,128]{3,2,1,0:T(8,128)}, u32[]{:S(2)}) copy-start(f32[4,18,16,128]{3,2,1,0:T(8,128)} %copy-done.3) | copy-start | bytes 1769476
  43.6 4.3 copy-start.25
  45.4 164.0 %all-gather.12.cloned.1.call-start = ((), (), s32[]{:S(2)}) async-start(), calls=%async_computation.2 | async-start | bytes 4866048 | tf_op jit(solution)/shard_map/all_gather | solution.py:115
  47.4 37.8 %copy-start.6 = (f32[16,16,128]{2,1,0:T(8,128)}, f32[16,16,128]{2,1,0:T(8,128)S(1)}, u32[]{:S(2)}) copy-start(f32[16,16,128]{2,1,0:T(8,128)S(1)} %get-tuple-element.57) | copy-start | bytes 393220
  50.5 7.3 %collective-permute-start.7 = (f32[4,1,16,128]{3,2,1,0:T(8,128)S(1)}, f32[4,1,16,128]{3,2,1,0:T(8,128)S(1)}, u32[]{:S(2)}, u32[]{:S(2)}) collective-permute-start(f32[4,1,16,128]{3,2,1,0:T(8,128)S(1)} %get-tuple-element.53), channel_id=1, source_target_pairs={{0,8},{8,16},{16,24},{24,32},{32,40},{40,48},{48,56},{56,64},{64,7... | collective-permute-start | bytes 98312 | tf_op jit(solution)/shard_map/ppermute | solution.py:18
  50.6 7.3 %collective-permute-start.6 = (f32[4,1,16,128]{3,2,1,0:T(8,128)S(1)}, f32[4,1,16,128]{3,2,1,0:T(8,128)S(1)}, u32[]{:S(2)}, u32[]{:S(2)}) collective-permute-start(f32[4,1,16,128]{3,2,1,0:T(8,128)S(1)} %get-tuple-element.54), channel_id=1, source_target_pairs={{8,0},{16,8},{24,16},{32,24},{40,32},{48,40},{56,48},{64,56},{72,6... | collective-permute-start | bytes 98312 | tf_op jit(solution)/shard_map/ppermute | solution.py:19
  57.8 3.8 copy-start.16
  57.8 3.7 copy-start.17
  57.9 1.7 collective-permute-start.8
  58.0 3.5 collective-permute-start.9
  59.7 1.9 copy-start.12
  66.9 12.2 %collective-permute-start.10 = (f32[4,18,18,1]{2,0,3,1:T(4,128)}, f32[4,18,18,1]{2,0,3,1:T(4,128)S(1)}, u32[]{:S(2)}, u32[]{:S(2)}) collective-permute-start(f32[4,18,18,1]{2,0,3,1:T(4,128)} %copy.602), channel_id=1, source_target_pairs={{1,0},{3,2},{5,4},{7,6},{9,8},{11,10},{13,12},{15,14},{17,16},{19,... | collective-permute-start | bytes 15560 | tf_op jit(solution)/shard_map/ppermute | solution.py:19
  68.2 10.3 %collective-permute-start.11 = (f32[4,18,18,1]{2,0,3,1:T(4,128)}, f32[4,18,18,1]{2,0,3,1:T(4,128)S(1)}, u32[]{:S(2)}, u32[]{:S(2)}) collective-permute-start(f32[4,18,18,1]{2,0,3,1:T(4,128)} %copy.604), channel_id=1, source_target_pairs={{0,1},{2,3},{4,5},{6,7},{8,9},{10,11},{12,13},{14,15},{16,17},{18,... | collective-permute-start | bytes 15560 | tf_op jit(solution)/shard_map/ppermute | solution.py:18
  80.6 3.4 copy-start.23
  80.8 3.8 copy-start.27
  83.6 208.7 %all-gather.10.cloned.1.call-start = ((), (), s32[]{:S(2)}) async-start(), calls=%async_computation.1 | async-start | bytes 4866048 | tf_op jit(solution)/shard_map/all_gather | solution.py:115
  87.2 7.8 %collective-permute-start.13 = (f32[4,1,16,128]{3,2,1,0:T(8,128)S(1)}, f32[4,1,16,128]{3,2,1,0:T(8,128)S(1)}, u32[]{:S(2)}, u32[]{:S(2)}) collective-permute-start(f32[4,1,16,128]{3,2,1,0:T(8,128)S(1)} %get-tuple-element.51), channel_id=1, source_target_pairs={{0,8},{8,16},{16,24},{24,32},{32,40},{40,48},{48,56},{56,64},{64,7... | collective-permute-start | bytes 98312 | tf_op jit(solution)/shard_map/ppermute | solution.py:18
  87.2 7.9 %collective-permute-start.12 = (f32[4,1,16,128]{3,2,1,0:T(8,128)S(1)}, f32[4,1,16,128]{3,2,1,0:T(8,128)S(1)}, u32[]{:S(2)}, u32[]{:S(2)}) collective-permute-start(f32[4,1,16,128]{3,2,1,0:T(8,128)S(1)} %get-tuple-element.52), channel_id=1, source_target_pairs={{8,0},{16,8},{24,16},{32,24},{40,32},{48,40},{56,48},{64,56},{72,6... | collective-permute-start | bytes 98312 | tf_op jit(solution)/shard_map/ppermute | solution.py:19
  94.9 15.4 %copy-start.14 = (f32[4,1,16,128]{3,2,1,0:T(8,128)}, f32[4,1,16,128]{3,2,1,0:T(8,128)S(1)}, u32[]{:S(2)}) copy-start(f32[4,1,16,128]{3,2,1,0:T(8,128)S(1)} %collective-permute-done.13) | copy-start | bytes 98308
  95.2 15.2 %copy-start.15 = (f32[4,1,16,128]{3,2,1,0:T(8,128)}, f32[4,1,16,128]{3,2,1,0:T(8,128)S(1)}, u32[]{:S(2)}) copy-start(f32[4,1,16,128]{3,2,1,0:T(8,128)S(1)} %collective-permute-done.12) | copy-start | bytes 98308
  95.2 1.7 collective-permute-start.14
  95.3 3.5 collective-permute-start.15
  98.8 11.5 %copy-start.8 = (f32[4,18,1,128]{3,2,1,0:T(1,128)}, f32[4,18,1,128]{3,2,1,0:T(1,128)S(1)}, u32[]{:S(2)}) copy-start(f32[4,18,1,128]{3,2,1,0:T(1,128)S(1)} %copy.609) | copy-start | bytes 110596
  102.5 15.3 %collective-permute-start.16 = (f32[4,18,18,1]{2,0,3,1:T(4,128)S(1)}, f32[4,18,18,1]{2,0,3,1:T(4,128)S(1)}, u32[]{:S(2)}, u32[]{:S(2)}) collective-permute-start(f32[4,18,18,1]{2,0,3,1:T(4,128)S(1)} %copy.612), channel_id=1, source_target_pairs={{1,0},{3,2},{5,4},{7,6},{9,8},{11,10},{13,12},{15,14},{17,16},{19,... | collective-permute-start | bytes 15560 | tf_op jit(solution)/shard_map/ppermute | solution.py:19
  103.8 12.6 %collective-permute-start.17 = (f32[4,18,18,1]{2,0,3,1:T(4,128)S(1)}, f32[4,18,18,1]{2,0,3,1:T(4,128)S(1)}, u32[]{:S(2)}, u32[]{:S(2)}) collective-permute-start(f32[4,18,18,1]{2,0,3,1:T(4,128)S(1)} %copy.614), channel_id=1, source_target_pairs={{0,1},{2,3},{4,5},{6,7},{8,9},{10,11},{12,13},{14,15},{16,17},{18,... | collective-permute-start | bytes 15560 | tf_op jit(solution)/shard_map/ppermute | solution.py:18
  119.7 4.3 copy-start
  124.7 101.5 %collective-permute-start.19 = (f32[4,1,16,128]{3,2,1,0:T(8,128)}, f32[4,1,16,128]{3,2,1,0:T(8,128)}, u32[]{:S(2)}, u32[]{:S(2)}) collective-permute-start(f32[4,1,16,128]{3,2,1,0:T(8,128)} %get-tuple-element.18), channel_id=1, source_target_pairs={{0,8},{8,16},{16,24},{24,32},{32,40},{40,48},{48,56},{56,64},{64,7... | collective-permute-start | bytes 98312 | tf_op jit(solution)/shard_map/ppermute | solution.py:18
  124.9 101.4 %collective-permute-start.18 = (f32[4,1,16,128]{3,2,1,0:T(8,128)}, f32[4,1,16,128]{3,2,1,0:T(8,128)}, u32[]{:S(2)}, u32[]{:S(2)}) collective-permute-start(f32[4,1,16,128]{3,2,1,0:T(8,128)} %get-tuple-element.19), channel_id=1, source_target_pairs={{8,0},{16,8},{24,16},{32,24},{40,32},{48,40},{56,48},{64,56},{72,6... | collective-permute-start | bytes 98312 | tf_op jit(solution)/shard_map/ppermute | solution.py:19
  226.2 11.3 %copy-start.5 = (f32[4,1024]{0,1:T(8,128)S(1)}, f32[4,1024]{0,1:T(8,128)}, u32[]{:S(2)}) copy-start(f32[4,1024]{0,1:T(8,128)} %copy.647) | copy-start | bytes 49156
  231.9 18.4 %collective-permute-start.21 = (f32[4,1,16,128]{3,2,1,0:T(8,128)S(1)}, f32[4,1,16,128]{3,2,1,0:T(8,128)S(1)}, u32[]{:S(2)}, u32[]{:S(2)}) collective-permute-start(f32[4,1,16,128]{3,2,1,0:T(8,128)S(1)} %get-tuple-element.16), channel_id=1, source_target_pairs={{0,8},{8,16},{16,24},{24,32},{32,40},{40,48},{48,56},{56,64},{64,7... | collective-permute-start | bytes 98312 | tf_op jit(solution)/shard_map/ppermute | solution.py:18
  232.2 18.1 %collective-permute-start.20 = (f32[4,1,16,128]{3,2,1,0:T(8,128)S(1)}, f32[4,1,16,128]{3,2,1,0:T(8,128)}, u32[]{:S(2)}, u32[]{:S(2)}) collective-permute-start(f32[4,1,16,128]{3,2,1,0:T(8,128)S(1)} %get-tuple-element.17), channel_id=1, source_target_pairs={{8,0},{16,8},{24,16},{32,24},{40,32},{48,40},{56,48},{64,56},{72,6... | collective-permute-start | bytes 98312 | tf_op jit(solution)/shard_map/ppermute | solution.py:19
  258.5 55.1 %collective-permute-start.23 = (f32[4,1,16,128]{3,2,1,0:T(8,128)}, f32[4,1,16,128]{3,2,1,0:T(8,128)S(1)}, u32[]{:S(2)}, u32[]{:S(2)}) collective-permute-start(f32[4,1,16,128]{3,2,1,0:T(8,128)} %get-tuple-element.14), channel_id=1, source_target_pairs={{0,8},{8,16},{16,24},{24,32},{32,40},{40,48},{48,56},{56,64},{64,7... | collective-permute-start | bytes 98312 | tf_op jit(solution)/shard_map/ppermute | solution.py:18
  258.5 55.1 %collective-permute-start.22 = (f32[4,1,16,128]{3,2,1,0:T(8,128)}, f32[4,1,16,128]{3,2,1,0:T(8,128)}, u32[]{:S(2)}, u32[]{:S(2)}) collective-permute-start(f32[4,1,16,128]{3,2,1,0:T(8,128)} %get-tuple-element.15), channel_id=1, source_target_pairs={{8,0},{16,8},{24,16},{32,24},{40,32},{48,40},{56,48},{64,56},{72,6... | collective-permute-start | bytes 98312 | tf_op jit(solution)/shard_map/ppermute | solution.py:19
  372.6 5.7 %copy-start.19 = (f32[4,18,18,1]{2,0,3,1:T(4,128)S(1)}, f32[4,18,18,1]{2,0,3,1:T(4,128)}, u32[]{:S(2)}) copy-start(f32[4,18,18,1]{2,0,3,1:T(4,128)} %copy-done.18) | copy-start | bytes 15556
  372.6 6.3 %copy-start.21 = (f32[4,18,18,1]{2,0,3,1:T(4,128)S(1)}, f32[4,18,18,1]{2,0,3,1:T(4,128)}, u32[]{:S(2)}) copy-start(f32[4,18,18,1]{2,0,3,1:T(4,128)} %copy-done.20) | copy-start | bytes 15556
  372.6 6.9 %copy-start.7 = (f32[16,16,128]{2,1,0:T(8,128)S(1)}, f32[16,16,128]{2,1,0:T(8,128)}, u32[]{:S(2)}) copy-start(f32[16,16,128]{2,1,0:T(8,128)} %copy-done.6) | copy-start | bytes 393220
  372.6 6.9 %copy-start.9 = (f32[4,18,1,128]{3,2,1,0:T(1,128)S(1)}, f32[4,18,1,128]{3,2,1,0:T(1,128)}, u32[]{:S(2)}) copy-start(f32[4,18,1,128]{3,2,1,0:T(1,128)} %copy-done.8) | copy-start | bytes 110596
  372.6 98.3 %all-to-all-start = ((f32[32,1,4,8192]{3,2,1,0:T(4,128)}), f32[32,1,4,8192]{3,2,1,0:T(4,128)}, u32[]{:S(2)}, u32[]{:S(2)}) async-start(f32[32,1,4,8192]{3,2,1,0:T(4,128)} %stack.183), calls=%async_computation | async-start | bytes 8388608 | tf_op jit(solution)/shard_map/all_to_all | solution.py:125
  (10 other events, 8.4 us)
Sparse Core Ops, SparseCore 0:
  45.5 81.0 all-gather.13
  129.2 80.1 all-gather.11
  211.9 80.3 all-gather.9
